TPU v7x, 256 devices: a whole 4x4x8 slice. The times are simulated.
256 devices in a mesh: blk: 64 (over x, z_lo, y), rep: 4 (over z_hi, core).
Axes of the slice: x: 4, y: 4, z: 8 (z_hi: 2, z_lo: 4; z = z_hi * 4 + z_lo), core: 2. Of those that a mesh axis runs over, the one named last changes fastest.
Arguments:
- node_feats: float32 [32768, 256], P('blk'), may hold values from -6 to 6
- operator_tiles: float32 [256, 16, 128, 128], P('blk', 'rep'), may hold values from -0.125 to 0.125
- tile_cols: int32 [256, 16], P('blk', 'rep'), may hold values from 0 to 255, as said below
- weight: float32 [256, 256], replicated, may hold values from -0.375 to 0.375
- layer_bias: float32 [256], replicated, may hold values from -3 to 3
- cotangent: float32 [32768, 256], P(('blk', 'rep')), may hold values from -6 to 6
Outputs:
- layer_out: float32 [32768, 256], P(('blk', 'rep'))
- grad_feats: float32 [32768, 256], P(('blk', 'rep'))
- grad_weight: float32 [256, 256], replicated
- grad_bias: float32 [256], replicated
Inputs may be any that keep to these rules, and one draw needn't show every extreme that they name: `tile_cols`: owner of block j is j // 4, among 64 owners on a closed cycle. Slots r * 4 to (r + 1) * 4 - 1 of row block i name blocks whose owner lies at cycle distance (owner of i minus owner of the column, modulo the number of owners) from r * 16 to (r + 1) * 16 - 1. Slot 0 of row block i names block i itself. Entries may repeat within a row block.
All inputs are finite; a program needn't handle non-finite values.
Results may differ from a plain program's by a relative error of at most 0.0003.
Values sent between devices are 32-bit elements; how exact they have to be, the bound alone decides.
No kernel may reach another device: no remote copies, remote signals or barrier semaphores. Data moves between devices by JAX's collectives and lax.ppermute only.
A program may use at most 64 MiB of HBM per device.

v0:
```python
import math
import jax
import jax.numpy as jnp
from jax import lax
from jax.sharding import PartitionSpec as P

TOP_PRECISION = lax.Precision.HIGHEST


def shifted_2(value, axis, steps):
    count = lax.axis_size(axis)
    pairs = [(source, (source + steps) % count) for source in range(count)]
    return lax.ppermute(value, axis, pairs)


def body(node_feats, operator_tiles, tile_cols, weight, layer_bias, cotangent):
    cycle_size = lax.axis_size("blk")
    rep_size = lax.axis_size("rep")
    window = cycle_size // rep_size
    position = lax.axis_index("blk")
    replica = lax.axis_index("rep")
    offset = replica * window
    blocks, slot_count, tile_size, _ = operator_tiles.shape
    width = node_feats.shape[1]
    row_count = blocks * tile_size
    owners = tile_cols // blocks
    within = tile_cols % blocks
    distance = jnp.mod(position - owners, cycle_size) - offset
    columns = jnp.arange(blocks, dtype=jnp.int32)
    sections = jnp.arange(window, dtype=jnp.int32)
    chosen = (
        (distance[:, :, None, None] == sections[None, None, :, None])
        & (within[:, :, None, None] == columns[None, None, None, :])
    ).astype(jnp.float32)

    def reshape_to_blocks(rows):
        return rows.reshape(blocks, tile_size, width)

    def store(stacked, section_no, current):
        return lax.dynamic_update_index_in_dim(stacked, reshape_to_blocks(current), section_no, 0)

    aligned = node_feats
    for bit_pos in range(rep_size.bit_length() - 1):
        shifted = shifted_2(aligned, "blk", window << bit_pos)
        aligned = jnp.where((replica >> bit_pos) % 2 == 1, shifted, aligned)
    empty = jnp.zeros((window, blocks, tile_size, width), jnp.float32)

    def advance(section_no, loop_state):
        current, stacked = loop_state
        current = shifted_2(current, "blk", 1)
        return (current, store(stacked, section_no, current))

    _, received = lax.fori_loop(1, window, advance, (aligned, store(empty, 0, aligned)))
    selected_tiles = jnp.einsum("iksc,scbd->ikbd", chosen, received, precision=TOP_PRECISION)
    partial_aggregate = jnp.einsum(
        "uzrj,uzje->ure", operator_tiles, selected_tiles, precision=TOP_PRECISION
    ).reshape(row_count, width)
    aggregated = lax.psum_scatter(partial_aggregate, "rep", scatter_dimension=0, tiled=True)
    pre_act = jnp.dot(aggregated, weight, precision=TOP_PRECISION) + layer_bias
    negative = jnp.minimum(pre_act, 0.0)
    layer_out = jnp.where(pre_act > 0, pre_act, jnp.expm1(negative))
    grad_pre = cotangent * jnp.where(pre_act > 0, 1.0, jnp.exp(negative))
    grad_scale = 1.0 / math.sqrt(row_count * cycle_size)
    grad_weight = (
        jnp.einsum("rd,re->de", aggregated, grad_pre, precision=TOP_PRECISION) * grad_scale
    )
    grad_bias = jnp.sum(grad_pre, axis=0) * grad_scale
    grad_weight, grad_bias = lax.psum((grad_weight, grad_bias), ("blk", "rep"))
    grad_hidden = jnp.einsum("re,de->rd", grad_pre, weight, precision=TOP_PRECISION)
    hidden_gradient = lax.all_gather(grad_hidden, "rep", axis=0, tiled=True)
    slot_terms = jnp.einsum(
        "xszt,xzc->xstc",
        operator_tiles,
        reshape_to_blocks(hidden_gradient),
        precision=TOP_PRECISION,
    )
    sorted_terms = jnp.einsum("iksc,ikbd->scbd", chosen, slot_terms, precision=TOP_PRECISION)

    def adjoint_term(section_no):
        return lax.dynamic_index_in_dim(sorted_terms, section_no, 0, keepdims=False).reshape(
            row_count, width
        )

    def retreat(counter, running):
        moved = shifted_2(running, "blk", -1)
        return moved + adjoint_term(window - 1 - counter)

    adjoint = lax.fori_loop(1, window, retreat, adjoint_term(window - 1))
    for bit_pos in range(rep_size.bit_length() - 1):
        returned = shifted_2(adjoint, "blk", -(window << bit_pos))
        adjoint = jnp.where((replica >> bit_pos) % 2 == 1, returned, adjoint)
    grad_feats = lax.psum_scatter(adjoint, "rep", scatter_dimension=0, tiled=True)
    return (layer_out, grad_feats, grad_weight, grad_bias)


def solution(mesh):
    return jax.shard_map(
        body,
        mesh=mesh,
        in_specs=(
            P("blk", None),
            P("blk", "rep", None, None),
            P("blk", "rep"),
            P(),
            P(),
            P(("blk", "rep"), None),
        ),
        out_specs=(P(("blk", "rep"), None), P(("blk", "rep"), None), P(), P()),
        check_vma=False,
    )
```

profile of v0, /device:TPU:1, one launch (start us, length us, event | category | flops | bytes accessed | tf_op | source)
XLA Modules:
  0.0 966.0 jit_solution(15077650085938543299)
XLA Ops:
  9.3 10.8 %collective-permute-done.2 = f32[512,256]{1,0:T(8,128)S(1)} collective-permute-done((f32[512,256]{1,0:T(8,128)}, f32[512,256]{1,0:T(8,128)S(1)}, u32[]{:S(2)}, u32[]{:S(2)}) %collective-permute-start.2) | collective-permute-done | bytes 524320 | tf_op jit(solution)/shard_map/ppermute | solution.py:13
  20.2 3.8 collective-permute-start.3
  24.8 7.8 collective-permute-done.3
  32.7 4.2 dynamic_update_slice.11
  37.0 259.1 %while.30 = (s32[]{:T(128)}, f32[512,256]{1,0:T(8,128)S(1)}, f32[16,4,128,256]{3,2,1,0:T(8,128)}, s32[]{:T(128)}, s32[]{:T(128)}, /*index=5*/s32[]{:T(128)}) while((s32[]{:T(128)}, f32[512,256]{1,0:T(8,128)S(1)}, f32[16,4,128,256]{3,2,1,0:T(8,128)}, s32[]{:T(128)}, s32[]{:T(128)}, /*index=5*/s32[]{:T(128)}) %tuple.67), condition=%wide.region_1.2_spmd, body=%wide.region_0.1_spmd.sunk | while | flops 5 | bytes 4194459 | solution.py:53
  37.0 3.5 collective-permute-start
  40.4 15.2 %collective-permute-done = f32[512,256]{1,0:T(8,128)S(1)} collective-permute-done((f32[512,256]{1,0:T(8,128)S(1)}, f32[512,256]{1,0:T(8,128)S(1)}, u32[]{:S(2)}, u32[]{:S(2)}) %collective-permute-start) | collective-permute-done | bytes 524320 | tf_op jit(solution)/shard_map/while/body/eval_jaxpr/ppermute | solution.py:13
  56.6 15.3 %collective-permute-done = f32[512,256]{1,0:T(8,128)S(1)} collective-permute-done((f32[512,256]{1,0:T(8,128)S(1)}, f32[512,256]{1,0:T(8,128)S(1)}, u32[]{:S(2)}, u32[]{:S(2)}) %collective-permute-start) | collective-permute-done | bytes 524320 | tf_op jit(solution)/shard_map/while/body/eval_jaxpr/ppermute | solution.py:13
  72.9 14.3 %collective-permute-done = f32[512,256]{1,0:T(8,128)S(1)} collective-permute-done((f32[512,256]{1,0:T(8,128)S(1)}, f32[512,256]{1,0:T(8,128)S(1)}, u32[]{:S(2)}, u32[]{:S(2)}) %collective-permute-start) | collective-permute-done | bytes 524320 | tf_op jit(solution)/shard_map/while/body/eval_jaxpr/ppermute | solution.py:13
  88.2 14.0 %collective-permute-done = f32[512,256]{1,0:T(8,128)S(1)} collective-permute-done((f32[512,256]{1,0:T(8,128)S(1)}, f32[512,256]{1,0:T(8,128)S(1)}, u32[]{:S(2)}, u32[]{:S(2)}) %collective-permute-start) | collective-permute-done | bytes 524320 | tf_op jit(solution)/shard_map/while/body/eval_jaxpr/ppermute | solution.py:13
  103.2 14.0 %collective-permute-done = f32[512,256]{1,0:T(8,128)S(1)} collective-permute-done((f32[512,256]{1,0:T(8,128)S(1)}, f32[512,256]{1,0:T(8,128)S(1)}, u32[]{:S(2)}, u32[]{:S(2)}) %collective-permute-start) | collective-permute-done | bytes 524320 | tf_op jit(solution)/shard_map/while/body/eval_jaxpr/ppermute | solution.py:13
  118.3 14.0 %collective-permute-done = f32[512,256]{1,0:T(8,128)S(1)} collective-permute-done((f32[512,256]{1,0:T(8,128)S(1)}, f32[512,256]{1,0:T(8,128)S(1)}, u32[]{:S(2)}, u32[]{:S(2)}) %collective-permute-start) | collective-permute-done | bytes 524320 | tf_op jit(solution)/shard_map/while/body/eval_jaxpr/ppermute | solution.py:13
  133.3 14.0 %collective-permute-done = f32[512,256]{1,0:T(8,128)S(1)} collective-permute-done((f32[512,256]{1,0:T(8,128)S(1)}, f32[512,256]{1,0:T(8,128)S(1)}, u32[]{:S(2)}, u32[]{:S(2)}) %collective-permute-start) | collective-permute-done | bytes 524320 | tf_op jit(solution)/shard_map/while/body/eval_jaxpr/ppermute | solution.py:13
  148.3 14.5 %collective-permute-done = f32[512,256]{1,0:T(8,128)S(1)} collective-permute-done((f32[512,256]{1,0:T(8,128)S(1)}, f32[512,256]{1,0:T(8,128)S(1)}, u32[]{:S(2)}, u32[]{:S(2)}) %collective-permute-start) | collective-permute-done | bytes 524320 | tf_op jit(solution)/shard_map/while/body/eval_jaxpr/ppermute | solution.py:13
  163.8 15.6 %collective-permute-done = f32[512,256]{1,0:T(8,128)S(1)} collective-permute-done((f32[512,256]{1,0:T(8,128)S(1)}, f32[512,256]{1,0:T(8,128)S(1)}, u32[]{:S(2)}, u32[]{:S(2)}) %collective-permute-start) | collective-permute-done | bytes 524320 | tf_op jit(solution)/shard_map/while/body/eval_jaxpr/ppermute | solution.py:13
  180.4 16.7 %collective-permute-done = f32[512,256]{1,0:T(8,128)S(1)} collective-permute-done((f32[512,256]{1,0:T(8,128)S(1)}, f32[512,256]{1,0:T(8,128)S(1)}, u32[]{:S(2)}, u32[]{:S(2)}) %collective-permute-start) | collective-permute-done | bytes 524320 | tf_op jit(solution)/shard_map/while/body/eval_jaxpr/ppermute | solution.py:13
  198.1 17.7 %collective-permute-done = f32[512,256]{1,0:T(8,128)S(1)} collective-permute-done((f32[512,256]{1,0:T(8,128)S(1)}, f32[512,256]{1,0:T(8,128)S(1)}, u32[]{:S(2)}, u32[]{:S(2)}) %collective-permute-start) | collective-permute-done | bytes 524320 | tf_op jit(solution)/shard_map/while/body/eval_jaxpr/ppermute | solution.py:13
  216.9 18.9 %collective-permute-done = f32[512,256]{1,0:T(8,128)S(1)} collective-permute-done((f32[512,256]{1,0:T(8,128)S(1)}, f32[512,256]{1,0:T(8,128)S(1)}, u32[]{:S(2)}, u32[]{:S(2)}) %collective-permute-start) | collective-permute-done | bytes 524320 | tf_op jit(solution)/shard_map/while/body/eval_jaxpr/ppermute | solution.py:13
  236.7 19.7 %collective-permute-done = f32[512,256]{1,0:T(8,128)S(1)} collective-permute-done((f32[512,256]{1,0:T(8,128)S(1)}, f32[512,256]{1,0:T(8,128)S(1)}, u32[]{:S(2)}, u32[]{:S(2)}) %collective-permute-start) | collective-permute-done | bytes 524320 | tf_op jit(solution)/shard_map/while/body/eval_jaxpr/ppermute | solution.py:13
  257.4 18.8 %collective-permute-done = f32[512,256]{1,0:T(8,128)S(1)} collective-permute-done((f32[512,256]{1,0:T(8,128)S(1)}, f32[512,256]{1,0:T(8,128)S(1)}, u32[]{:S(2)}, u32[]{:S(2)}) %collective-permute-start) | collective-permute-done | bytes 524320 | tf_op jit(solution)/shard_map/while/body/eval_jaxpr/ppermute | solution.py:13
  277.1 17.8 %collective-permute-done = f32[512,256]{1,0:T(8,128)S(1)} collective-permute-done((f32[512,256]{1,0:T(8,128)S(1)}, f32[512,256]{1,0:T(8,128)S(1)}, u32[]{:S(2)}, u32[]{:S(2)}) %collective-permute-start) | collective-permute-done | bytes 524320 | tf_op jit(solution)/shard_map/while/body/eval_jaxpr/ppermute | solution.py:13
  296.1 13.0 %fusion = f32[4,4,128,256,1]{3,1,4,2,0:T(4,128)S(1)} fusion(f32[16,4,128,256,1]{3,2,1,0,4:T(8,128)} %bitcast.48, pred[4,4,4]{1,0,2:T(4,128)(4,1)S(1)} %iota_compare_fusion, pred[4,4,16]{2,1,0:T(4,128)(4,1)S(1)} %iota_compare_fusion.1), kind=kOutput, calls=%fused_computation.3 | convolution fusion | flops 402654208 | bytes 10486080 | tf_op jit(solution)/shard_map/iksc,scbd->ikbd/dot_general | solution.py:54
  311.9 55.4 %reduce-scatter.3.cloned.1.call-done = f32[128,256]{1,0:T(8,128)} async-done(((f32[512,256]{1,0:T(8,128)}), f32[128,256]{1,0:T(8,128)}) %reduce-scatter.3.cloned.1.call-update) | async-done | bytes 131088 | tf_op jit(solution)/shard_map/reduce_scatter | solution.py:58
  369.5 13.7 %all_gather.3 = f32[512,256]{1,0:T(8,128)S(1)} all-gather(f32[128,256]{1,0:T(8,128)S(1)} %fusion.16), channel_id=1, replica_groups=mesh['blk'=64,'rep'=4] {'rep'}, dimensions={0}, use_global_device_ids=true | all-gather | bytes 655360 | tf_op jit(solution)/shard_map/all_gather | solution.py:70
  387.1 5.9 convolution_bitcast_fusion
  393.7 2.6 copy-done.2
  396.3 242.4 %while.31 = (s32[]{:T(128)}, f32[512,256]{1,0:T(8,128)S(1)}, f32[16,4,128,256]{3,0,2,1:T(8,128)}, s32[]{:T(128)}, s32[]{:T(128)}, /*index=5*/s32[]{:T(128)}, s32[]{:T(128)}) while((s32[]{:T(128)}, f32[512,256]{1,0:T(8,128)S(1)}, f32[16,4,128,256]{3,0,2,1:T(8,128)}, s32[]{:T(128)}, s32[]{:T(128)}, /*index=5*/s32[]{:T(128)}, s32[]{:T(128)}) %tuple.81), condition=%wide.region_4.5_spmd, body=%wide.region_3.4_spmd.sunk | while | flops 131078 | bytes 5767335 | solution.py:88
  396.3 3.7 collective-permute-start.1
  400.0 2.5 constant_dynamic-slice_fusion.2
  402.6 8.6 collective-permute-done.1
  411.3 8.3 collective-permute-start.1
  419.6 2.5 constant_dynamic-slice_fusion.2
  422.2 7.7 collective-permute-done.1
  429.9 8.3 collective-permute-start.1
  440.8 6.7 collective-permute-done.1
  447.7 8.3 collective-permute-start.1
  458.5 5.8 collective-permute-done.1
  464.5 8.3 collective-permute-start.1
  475.3 4.9 collective-permute-done.1
  480.3 8.3 collective-permute-start.1
  491.2 4.0 collective-permute-done.1
  495.3 8.3 collective-permute-start.1
  506.2 3.5 collective-permute-done.1
  509.8 8.0 collective-permute-start.1
  520.4 3.5 collective-permute-done.1
  524.0 8.0 collective-permute-start.1
  534.6 3.5 collective-permute-done.1
  538.2 8.0 collective-permute-start.1
  548.8 3.5 collective-permute-done.1
  552.4 8.0 collective-permute-start.1
  563.0 4.4 collective-permute-done.1
  567.5 8.0 collective-permute-start.1
  578.1 5.5 collective-permute-done.1
  583.7 8.0 collective-permute-start.1
  594.3 6.6 collective-permute-done.1
  600.9 8.0 collective-permute-start.1
  611.5 7.6 collective-permute-done.1
  619.3 8.0 collective-permute-start.1
  629.9 8.7 collective-permute-done.1
  638.8 8.3 collective-permute-done.4
  648.5 8.3 collective-permute-done.5
  657.7 94.6 %psum.15 = f32[256]{0:T(256)} all-reduce(f32[256]{0:T(256)S(1)} %broadcast_multiply_fusion), channel_id=1, replica_groups=mesh['blk'=64,'rep'=4] {'blk','rep'}, use_global_device_ids=true, to_apply=%region_8.9 | all-reduce | flops 256 | bytes 2048 | tf_op jit(solution)/shard_map/psum | solution.py:68
  752.3 162.6 %all-reduce.3.cloned.1.call-done = f32[256,256]{1,0:T(8,128)} async-done(((f32[256,256]{1,0:T(8,128)}), f32[256,256]{1,0:T(8,128)}) %all-reduce.3.cloned.1.call-update) | async-done | bytes 262160 | tf_op jit(solution)/shard_map/psum | solution.py:68
  914.9 42.9 %reduce-scatter.5.cloned.1.call-done = f32[128,256]{1,0:T(8,128)} async-done(((f32[512,256]{1,0:T(8,128)}), f32[128,256]{1,0:T(8,128)}) %reduce-scatter.5.cloned.1.call-update) | async-done | bytes 131088 | tf_op jit(solution)/shard_map/reduce_scatter | solution.py:92
  (124 shorter events, 65.8 us)
Async XLA Ops:
  7.2 301.9 %copy-start = (f32[4,4,128,128]{3,2,1,0:T(8,128)S(1)}, f32[4,4,128,128]{3,2,1,0:T(8,128)}, u32[]{:S(2)}) copy-start(f32[4,4,128,128]{3,2,1,0:T(8,128)} %param.11) | copy-start | bytes 3145732
  7.2 360.1 %reduce-scatter.3.cloned.1.call-start = ((), (), s32[]{:S(2)}) async-start(), calls=%async_computation.2 | async-start | bytes 655360 | tf_op jit(solution)/shard_map/reduce_scatter | solution.py:58
  7.2 12.9 %collective-permute-start.2 = (f32[512,256]{1,0:T(8,128)}, f32[512,256]{1,0:T(8,128)S(1)}, u32[]{:S(2)}, u32[]{:S(2)}) collective-permute-start(f32[512,256]{1,0:T(8,128)} %param.10), channel_id=1, source_target_pairs={{0,64},{4,68},{8,72},{12,76},{16,80},{20,84},{24,88},{28,92},{32,9... | collective-permute-start | bytes 1572872 | tf_op jit(solution)/shard_map/ppermute | solution.py:13
  20.2 12.4 %collective-permute-start.3 = (f32[512,256]{1,0:T(8,128)S(1)}, f32[512,256]{1,0:T(8,128)S(1)}, u32[]{:S(2)}, u32[]{:S(2)}) collective-permute-start(f32[512,256]{1,0:T(8,128)S(1)} %broadcast_select_fusion.1), channel_id=1, source_target_pairs={{0,128},{4,132},{8,136},{12,140},{16,144},{20,148},{24,152},{28,15... | collective-permute-start | bytes 1572872 | tf_op jit(solution)/shard_map/ppermute | solution.py:13
  37.0 18.7 %collective-permute-start = (f32[512,256]{1,0:T(8,128)S(1)}, f32[512,256]{1,0:T(8,128)S(1)}, u32[]{:S(2)}, u32[]{:S(2)}) collective-permute-start(f32[512,256]{1,0:T(8,128)S(1)} %get-tuple-element.223), channel_id=1, source_target_pairs={{0,4},{4,8},{8,12},{12,16},{16,20},{20,24},{24,28},{28,32},{32,36}... | collective-permute-start | bytes 1572872 | tf_op jit(solution)/shard_map/while/body/eval_jaxpr/ppermute | solution.py:13
  56.5 15.4 %collective-permute-start = (f32[512,256]{1,0:T(8,128)S(1)}, f32[512,256]{1,0:T(8,128)S(1)}, u32[]{:S(2)}, u32[]{:S(2)}) collective-permute-start(f32[512,256]{1,0:T(8,128)S(1)} %get-tuple-element.223), channel_id=1, source_target_pairs={{0,4},{4,8},{8,12},{12,16},{16,20},{20,24},{24,28},{28,32},{32,36}... | collective-permute-start | bytes 1572872 | tf_op jit(solution)/shard_map/while/body/eval_jaxpr/ppermute | solution.py:13
  72.8 14.4 %collective-permute-start = (f32[512,256]{1,0:T(8,128)S(1)}, f32[512,256]{1,0:T(8,128)S(1)}, u32[]{:S(2)}, u32[]{:S(2)}) collective-permute-start(f32[512,256]{1,0:T(8,128)S(1)} %get-tuple-element.223), channel_id=1, source_target_pairs={{0,4},{4,8},{8,12},{12,16},{16,20},{20,24},{24,28},{28,32},{32,36}... | collective-permute-start | bytes 1572872 | tf_op jit(solution)/shard_map/while/body/eval_jaxpr/ppermute | solution.py:13
  88.1 14.1 %collective-permute-start = (f32[512,256]{1,0:T(8,128)S(1)}, f32[512,256]{1,0:T(8,128)S(1)}, u32[]{:S(2)}, u32[]{:S(2)}) collective-permute-start(f32[512,256]{1,0:T(8,128)S(1)} %get-tuple-element.223), channel_id=1, source_target_pairs={{0,4},{4,8},{8,12},{12,16},{16,20},{20,24},{24,28},{28,32},{32,36}... | collective-permute-start | bytes 1572872 | tf_op jit(solution)/shard_map/while/body/eval_jaxpr/ppermute | solution.py:13
  103.2 14.1 %collective-permute-start = (f32[512,256]{1,0:T(8,128)S(1)}, f32[512,256]{1,0:T(8,128)S(1)}, u32[]{:S(2)}, u32[]{:S(2)}) collective-permute-start(f32[512,256]{1,0:T(8,128)S(1)} %get-tuple-element.223), channel_id=1, source_target_pairs={{0,4},{4,8},{8,12},{12,16},{16,20},{20,24},{24,28},{28,32},{32,36}... | collective-permute-start | bytes 1572872 | tf_op jit(solution)/shard_map/while/body/eval_jaxpr/ppermute | solution.py:13
  118.2 14.1 %collective-permute-start = (f32[512,256]{1,0:T(8,128)S(1)}, f32[512,256]{1,0:T(8,128)S(1)}, u32[]{:S(2)}, u32[]{:S(2)}) collective-permute-start(f32[512,256]{1,0:T(8,128)S(1)} %get-tuple-element.223), channel_id=1, source_target_pairs={{0,4},{4,8},{8,12},{12,16},{16,20},{20,24},{24,28},{28,32},{32,36}... | collective-permute-start | bytes 1572872 | tf_op jit(solution)/shard_map/while/body/eval_jaxpr/ppermute | solution.py:13
  133.2 14.1 %collective-permute-start = (f32[512,256]{1,0:T(8,128)S(1)}, f32[512,256]{1,0:T(8,128)S(1)}, u32[]{:S(2)}, u32[]{:S(2)}) collective-permute-start(f32[512,256]{1,0:T(8,128)S(1)} %get-tuple-element.223), channel_id=1, source_target_pairs={{0,4},{4,8},{8,12},{12,16},{16,20},{20,24},{24,28},{28,32},{32,36}... | collective-permute-start | bytes 1572872 | tf_op jit(solution)/shard_map/while/body/eval_jaxpr/ppermute | solution.py:13
  148.2 14.6 %collective-permute-start = (f32[512,256]{1,0:T(8,128)S(1)}, f32[512,256]{1,0:T(8,128)S(1)}, u32[]{:S(2)}, u32[]{:S(2)}) collective-permute-start(f32[512,256]{1,0:T(8,128)S(1)} %get-tuple-element.223), channel_id=1, source_target_pairs={{0,4},{4,8},{8,12},{12,16},{16,20},{20,24},{24,28},{28,32},{32,36}... | collective-permute-start | bytes 1572872 | tf_op jit(solution)/shard_map/while/body/eval_jaxpr/ppermute | solution.py:13
  163.7 15.7 %collective-permute-start = (f32[512,256]{1,0:T(8,128)S(1)}, f32[512,256]{1,0:T(8,128)S(1)}, u32[]{:S(2)}, u32[]{:S(2)}) collective-permute-start(f32[512,256]{1,0:T(8,128)S(1)} %get-tuple-element.223), channel_id=1, source_target_pairs={{0,4},{4,8},{8,12},{12,16},{16,20},{20,24},{24,28},{28,32},{32,36}... | collective-permute-start | bytes 1572872 | tf_op jit(solution)/shard_map/while/body/eval_jaxpr/ppermute | solution.py:13
  180.3 16.8 %collective-permute-start = (f32[512,256]{1,0:T(8,128)S(1)}, f32[512,256]{1,0:T(8,128)S(1)}, u32[]{:S(2)}, u32[]{:S(2)}) collective-permute-start(f32[512,256]{1,0:T(8,128)S(1)} %get-tuple-element.223), channel_id=1, source_target_pairs={{0,4},{4,8},{8,12},{12,16},{16,20},{20,24},{24,28},{28,32},{32,36}... | collective-permute-start | bytes 1572872 | tf_op jit(solution)/shard_map/while/body/eval_jaxpr/ppermute | solution.py:13
  198.1 17.8 %collective-permute-start = (f32[512,256]{1,0:T(8,128)S(1)}, f32[512,256]{1,0:T(8,128)S(1)}, u32[]{:S(2)}, u32[]{:S(2)}) collective-permute-start(f32[512,256]{1,0:T(8,128)S(1)} %get-tuple-element.223), channel_id=1, source_target_pairs={{0,4},{4,8},{8,12},{12,16},{16,20},{20,24},{24,28},{28,32},{32,36}... | collective-permute-start | bytes 1572872 | tf_op jit(solution)/shard_map/while/body/eval_jaxpr/ppermute | solution.py:13
  216.8 19.0 %collective-permute-start = (f32[512,256]{1,0:T(8,128)S(1)}, f32[512,256]{1,0:T(8,128)S(1)}, u32[]{:S(2)}, u32[]{:S(2)}) collective-permute-start(f32[512,256]{1,0:T(8,128)S(1)} %get-tuple-element.223), channel_id=1, source_target_pairs={{0,4},{4,8},{8,12},{12,16},{16,20},{20,24},{24,28},{28,32},{32,36}... | collective-permute-start | bytes 1572872 | tf_op jit(solution)/shard_map/while/body/eval_jaxpr/ppermute | solution.py:13
  236.6 19.7 %collective-permute-start = (f32[512,256]{1,0:T(8,128)S(1)}, f32[512,256]{1,0:T(8,128)S(1)}, u32[]{:S(2)}, u32[]{:S(2)}) collective-permute-start(f32[512,256]{1,0:T(8,128)S(1)} %get-tuple-element.223), channel_id=1, source_target_pairs={{0,4},{4,8},{8,12},{12,16},{16,20},{20,24},{24,28},{28,32},{32,36}... | collective-permute-start | bytes 1572872 | tf_op jit(solution)/shard_map/while/body/eval_jaxpr/ppermute | solution.py:13
  257.3 18.8 %collective-permute-start = (f32[512,256]{1,0:T(8,128)S(1)}, f32[512,256]{1,0:T(8,128)S(1)}, u32[]{:S(2)}, u32[]{:S(2)}) collective-permute-start(f32[512,256]{1,0:T(8,128)S(1)} %get-tuple-element.223), channel_id=1, source_target_pairs={{0,4},{4,8},{8,12},{12,16},{16,20},{20,24},{24,28},{28,32},{32,36}... | collective-permute-start | bytes 1572872 | tf_op jit(solution)/shard_map/while/body/eval_jaxpr/ppermute | solution.py:13
  277.0 17.9 %collective-permute-start = (f32[512,256]{1,0:T(8,128)S(1)}, f32[512,256]{1,0:T(8,128)S(1)}, u32[]{:S(2)}, u32[]{:S(2)}) collective-permute-start(f32[512,256]{1,0:T(8,128)S(1)} %get-tuple-element.223), channel_id=1, source_target_pairs={{0,4},{4,8},{8,12},{12,16},{16,20},{20,24},{24,28},{28,32},{32,36}... | collective-permute-start | bytes 1572872 | tf_op jit(solution)/shard_map/while/body/eval_jaxpr/ppermute | solution.py:13
  296.1 71.2 %copy-start.1 = (f32[128,256]{1,0:T(8,128)S(1)}, f32[128,256]{1,0:T(8,128)}, u32[]{:S(2)}) copy-start(f32[128,256]{1,0:T(8,128)} %param.15) | copy-start | bytes 393220
  296.1 71.2 %copy-start.3 = (f32[256,256]{1,0:T(8,128)S(1)}, f32[256,256]{1,0:T(8,128)}, u32[]{:S(2)}) copy-start(f32[256,256]{1,0:T(8,128)} %param.13) | copy-start | bytes 786436
  296.1 71.2 %copy-start.5 = (f32[256]{0:T(256)S(1)}, f32[256]{0:T(256)}, u32[]{:S(2)}) copy-start(f32[256]{0:T(256)} %param.14) | copy-start | bytes 3076
  311.6 603.3 %all-reduce.3.cloned.1.call-start = ((), (), s32[]{:S(2)}) async-start(), calls=%async_computation.4 | async-start | bytes 524288 | tf_op jit(solution)/shard_map/psum | solution.py:68
  393.1 3.2 copy-start.2
  396.3 250.9 %copy-start.4 = (f32[128,256]{1,0:T(8,128)S(1)}, f32[128,256]{1,0:T(8,128)}, u32[]{:S(2)}) copy-start(f32[128,256]{1,0:T(8,128)} %reduce-scatter.3.cloned.1.call-done) | copy-start | bytes 393220
  396.3 14.9 %collective-permute-start.1 = (f32[512,256]{1,0:T(8,128)S(1)}, f32[512,256]{1,0:T(8,128)S(1)}, u32[]{:S(2)}, u32[]{:S(2)}) collective-permute-start(f32[512,256]{1,0:T(8,128)S(1)} %get-tuple-element.242), channel_id=1, source_target_pairs={{0,252},{4,0},{8,4},{12,8},{16,12},{20,16},{24,20},{28,24},{32,28}... | collective-permute-start | bytes 1572872 | tf_op jit(solution)/shard_map/while/body/eval_jaxpr/ppermute | solution.py:13
  411.3 18.6 %collective-permute-start.1 = (f32[512,256]{1,0:T(8,128)S(1)}, f32[512,256]{1,0:T(8,128)S(1)}, u32[]{:S(2)}, u32[]{:S(2)}) collective-permute-start(f32[512,256]{1,0:T(8,128)S(1)} %get-tuple-element.242), channel_id=1, source_target_pairs={{0,252},{4,0},{8,4},{12,8},{16,12},{20,16},{24,20},{28,24},{32,28}... | collective-permute-start | bytes 1572872 | tf_op jit(solution)/shard_map/while/body/eval_jaxpr/ppermute | solution.py:13
  429.9 17.6 %collective-permute-start.1 = (f32[512,256]{1,0:T(8,128)S(1)}, f32[512,256]{1,0:T(8,128)S(1)}, u32[]{:S(2)}, u32[]{:S(2)}) collective-permute-start(f32[512,256]{1,0:T(8,128)S(1)} %get-tuple-element.242), channel_id=1, source_target_pairs={{0,252},{4,0},{8,4},{12,8},{16,12},{20,16},{24,20},{28,24},{32,28}... | collective-permute-start | bytes 1572872 | tf_op jit(solution)/shard_map/while/body/eval_jaxpr/ppermute | solution.py:13
  447.7 16.7 %collective-permute-start.1 = (f32[512,256]{1,0:T(8,128)S(1)}, f32[512,256]{1,0:T(8,128)S(1)}, u32[]{:S(2)}, u32[]{:S(2)}) collective-permute-start(f32[512,256]{1,0:T(8,128)S(1)} %get-tuple-element.242), channel_id=1, source_target_pairs={{0,252},{4,0},{8,4},{12,8},{16,12},{20,16},{24,20},{28,24},{32,28}... | collective-permute-start | bytes 1572872 | tf_op jit(solution)/shard_map/while/body/eval_jaxpr/ppermute | solution.py:13
  464.5 15.8 %collective-permute-start.1 = (f32[512,256]{1,0:T(8,128)S(1)}, f32[512,256]{1,0:T(8,128)S(1)}, u32[]{:S(2)}, u32[]{:S(2)}) collective-permute-start(f32[512,256]{1,0:T(8,128)S(1)} %get-tuple-element.242), channel_id=1, source_target_pairs={{0,252},{4,0},{8,4},{12,8},{16,12},{20,16},{24,20},{28,24},{32,28}... | collective-permute-start | bytes 1572872 | tf_op jit(solution)/shard_map/while/body/eval_jaxpr/ppermute | solution.py:13
  480.3 14.9 %collective-permute-start.1 = (f32[512,256]{1,0:T(8,128)S(1)}, f32[512,256]{1,0:T(8,128)S(1)}, u32[]{:S(2)}, u32[]{:S(2)}) collective-permute-start(f32[512,256]{1,0:T(8,128)S(1)} %get-tuple-element.242), channel_id=1, source_target_pairs={{0,252},{4,0},{8,4},{12,8},{16,12},{20,16},{24,20},{28,24},{32,28}... | collective-permute-start | bytes 1572872 | tf_op jit(solution)/shard_map/while/body/eval_jaxpr/ppermute | solution.py:13
  495.3 14.4 %collective-permute-start.1 = (f32[512,256]{1,0:T(8,128)S(1)}, f32[512,256]{1,0:T(8,128)S(1)}, u32[]{:S(2)}, u32[]{:S(2)}) collective-permute-start(f32[512,256]{1,0:T(8,128)S(1)} %get-tuple-element.242), channel_id=1, source_target_pairs={{0,252},{4,0},{8,4},{12,8},{16,12},{20,16},{24,20},{28,24},{32,28}... | collective-permute-start | bytes 1572872 | tf_op jit(solution)/shard_map/while/body/eval_jaxpr/ppermute | solution.py:13
  509.8 14.1 %collective-permute-start.1 = (f32[512,256]{1,0:T(8,128)S(1)}, f32[512,256]{1,0:T(8,128)S(1)}, u32[]{:S(2)}, u32[]{:S(2)}) collective-permute-start(f32[512,256]{1,0:T(8,128)S(1)} %get-tuple-element.242), channel_id=1, source_target_pairs={{0,252},{4,0},{8,4},{12,8},{16,12},{20,16},{24,20},{28,24},{32,28}... | collective-permute-start | bytes 1572872 | tf_op jit(solution)/shard_map/while/body/eval_jaxpr/ppermute | solution.py:13
  524.0 14.1 %collective-permute-start.1 = (f32[512,256]{1,0:T(8,128)S(1)}, f32[512,256]{1,0:T(8,128)S(1)}, u32[]{:S(2)}, u32[]{:S(2)}) collective-permute-start(f32[512,256]{1,0:T(8,128)S(1)} %get-tuple-element.242), channel_id=1, source_target_pairs={{0,252},{4,0},{8,4},{12,8},{16,12},{20,16},{24,20},{28,24},{32,28}... | collective-permute-start | bytes 1572872 | tf_op jit(solution)/shard_map/while/body/eval_jaxpr/ppermute | solution.py:13
  538.2 14.1 %collective-permute-start.1 = (f32[512,256]{1,0:T(8,128)S(1)}, f32[512,256]{1,0:T(8,128)S(1)}, u32[]{:S(2)}, u32[]{:S(2)}) collective-permute-start(f32[512,256]{1,0:T(8,128)S(1)} %get-tuple-element.242), channel_id=1, source_target_pairs={{0,252},{4,0},{8,4},{12,8},{16,12},{20,16},{24,20},{28,24},{32,28}... | collective-permute-start | bytes 1572872 | tf_op jit(solution)/shard_map/while/body/eval_jaxpr/ppermute | solution.py:13
  552.4 15.0 %collective-permute-start.1 = (f32[512,256]{1,0:T(8,128)S(1)}, f32[512,256]{1,0:T(8,128)S(1)}, u32[]{:S(2)}, u32[]{:S(2)}) collective-permute-start(f32[512,256]{1,0:T(8,128)S(1)} %get-tuple-element.242), channel_id=1, source_target_pairs={{0,252},{4,0},{8,4},{12,8},{16,12},{20,16},{24,20},{28,24},{32,28}... | collective-permute-start | bytes 1572872 | tf_op jit(solution)/shard_map/while/body/eval_jaxpr/ppermute | solution.py:13
  567.5 16.1 %collective-permute-start.1 = (f32[512,256]{1,0:T(8,128)S(1)}, f32[512,256]{1,0:T(8,128)S(1)}, u32[]{:S(2)}, u32[]{:S(2)}) collective-permute-start(f32[512,256]{1,0:T(8,128)S(1)} %get-tuple-element.242), channel_id=1, source_target_pairs={{0,252},{4,0},{8,4},{12,8},{16,12},{20,16},{24,20},{28,24},{32,28}... | collective-permute-start | bytes 1572872 | tf_op jit(solution)/shard_map/while/body/eval_jaxpr/ppermute | solution.py:13
  583.7 17.2 %collective-permute-start.1 = (f32[512,256]{1,0:T(8,128)S(1)}, f32[512,256]{1,0:T(8,128)S(1)}, u32[]{:S(2)}, u32[]{:S(2)}) collective-permute-start(f32[512,256]{1,0:T(8,128)S(1)} %get-tuple-element.242), channel_id=1, source_target_pairs={{0,252},{4,0},{8,4},{12,8},{16,12},{20,16},{24,20},{28,24},{32,28}... | collective-permute-start | bytes 1572872 | tf_op jit(solution)/shard_map/while/body/eval_jaxpr/ppermute | solution.py:13
  600.9 18.2 %collective-permute-start.1 = (f32[512,256]{1,0:T(8,128)S(1)}, f32[512,256]{1,0:T(8,128)S(1)}, u32[]{:S(2)}, u32[]{:S(2)}) collective-permute-start(f32[512,256]{1,0:T(8,128)S(1)} %get-tuple-element.242), channel_id=1, source_target_pairs={{0,252},{4,0},{8,4},{12,8},{16,12},{20,16},{24,20},{28,24},{32,28}... | collective-permute-start | bytes 1572872 | tf_op jit(solution)/shard_map/while/body/eval_jaxpr/ppermute | solution.py:13
  619.3 19.3 %collective-permute-start.1 = (f32[512,256]{1,0:T(8,128)S(1)}, f32[512,256]{1,0:T(8,128)S(1)}, u32[]{:S(2)}, u32[]{:S(2)}) collective-permute-start(f32[512,256]{1,0:T(8,128)S(1)} %get-tuple-element.242), channel_id=1, source_target_pairs={{0,252},{4,0},{8,4},{12,8},{16,12},{20,16},{24,20},{28,24},{32,28}... | collective-permute-start | bytes 1572872 | tf_op jit(solution)/shard_map/while/body/eval_jaxpr/ppermute | solution.py:13
  638.7 8.4 collective-permute-start.4
  647.1 9.6 collective-permute-start.5
  648.4 309.4 %reduce-scatter.5.cloned.1.call-start = ((), (), s32[]{:S(2)}) async-start(), calls=%async_computation.3 | async-start | bytes 655360 | tf_op jit(solution)/shard_map/reduce_scatter | solution.py:92
Sparse Core Ops, SparseCore 0:
  311.7 55.4 reduce-scatter.2
  648.5 266.3 all-reduce.2
  918.4 39.3 reduce-scatter.4
where the time goes:
time: 967 us; the launch traced here: 966 us
  waiting for transfers between devices  621 us (64%)
  starting transfers between devices  129 us (13%)
  blocking collectives  108 us (11%)
  local copies, waits for them, and re-layouts  63.2 us (7%)
  matrix products  26.6 us (3%)
  between operations  13.9 us (1%)
    ppermute x34, waiting for transfers between devices, shifted_2(): return lax.ppermute(value, axis, pairs)  361 us
    psum x1, waiting for transfers between devices, body(): grad_weight, grad_bias = lax.psum((grad_weight, grad_bias), ('blk', 'rep'))  163 us
    ppermute x34, starting transfers between devices, shifted_2(): return lax.ppermute(value, axis, pairs)  128 us
    psum x1, blocking collectives, body(): grad_weight, grad_bias = lax.psum((grad_weight, grad_bias), ('blk', 'rep'))  94.6 us
    reduce_scatter x1, waiting for transfers between devices, body(): lax.psum_scatter(partial_aggregate, 'rep', scatter_dimension=0, tiled=True)  55.4 us
    reduce_scatter x1, waiting for transfers between devices, body(): lax.psum_scatter(adjoint, 'rep', scatter_dimension=0, tiled=True)  42.9 us
    dynamic_slice x31, local copies, waits for them, and re-layouts, adjoint_term(): lax.dynamic_index_in_dim(sorted_terms, section_no, 0, keepdims=False)  39.3 us
  transfers between devices with their start and end apart: 37, of which 37 were waited for; matrix products, arithmetic and copies ran while one was open for 4% of the time, Pallas kernels for 0%

commit v1 on v0

--- a/solution.py
+++ b/solution.py
@@ -65,7 +65,7 @@
         jnp.einsum("rd,re->de", aggregated, grad_pre, precision=TOP_PRECISION) * grad_scale
     )
     grad_bias = jnp.sum(grad_pre, axis=0) * grad_scale
-    grad_weight, grad_bias = lax.psum((grad_weight, grad_bias), ("blk", "rep"))
+    grad_weight, grad_bias = lax.psum(lax.psum((grad_weight, grad_bias), "blk"), "rep")
     grad_hidden = jnp.einsum("re,de->rd", grad_pre, weight, precision=TOP_PRECISION)
     hidden_gradient = lax.all_gather(grad_hidden, "rep", axis=0, tiled=True)
     slot_terms = jnp.einsum(

time: 967 us -> 1530 us (1.58)
  waiting for transfers between devices: 621 us -> 1050 us
  blocking collectives: 108 us -> 237 us
    psum x1 -> x2, waiting for transfers between devices: 163 us -> 646 us  [the longest x1 646 us: body(): lax.psum((grad_weight, grad_bias), 'blk')]
    psum x1 -> x2, blocking collectives: 94.6 us -> 223 us  [the longest x1 159 us: body(): lax.psum((grad_weight, grad_bias), 'blk')]
    reduce_scatter x1, waiting for transfers between devices: 42.9 us -> 0.01 us  [body(): lax.psum_scatter(adjoint, 'rep', scatter_dimension=0, tiled=True)]
  transfers between devices with their start and end apart: 37 -> 38, of which waited for: 37 -> 35; matrix products, arithmetic and copies ran while one was open for 4% -> 3% of each run, Pallas kernels for 0% -> 0%
where the time goes in v1:
time: 1530 us
  waiting for transfers between devices  1050 us (69%)
  blocking collectives  237 us (15%)
  starting transfers between devices  129 us (8%)
  local copies, waits for them, and re-layouts  63.1 us (4%)
  matrix products  26.6 us (2%)
    psum x1, waiting for transfers between devices, body(): lax.psum((grad_weight, grad_bias), 'blk')  646 us
    ppermute x34, waiting for transfers between devices, shifted_2(): return lax.ppermute(value, axis, pairs)  352 us
    psum x1, blocking collectives, body(): lax.psum((grad_weight, grad_bias), 'blk')  159 us
    ppermute x34, starting transfers between devices, shifted_2(): return lax.ppermute(value, axis, pairs)  128 us
    psum x1, blocking collectives, body(): lax.psum(lax.psum((grad_weight, grad_bias), 'blk'), 'rep')  63.7 us
    reduce_scatter x1, waiting for transfers between devices, body(): lax.psum_scatter(partial_aggregate, 'rep', scatter_dimension=0, tiled=True)  55.4 us
    dynamic_slice x31, local copies, waits for them, and re-layouts, adjoint_term(): lax.dynamic_index_in_dim(sorted_terms, section_no, 0, keepdims=False)  39.3 us
  transfers between devices with their start and end apart: 38, of which 35 were waited for; matrix products, arithmetic and copies ran while one was open for 3% of the time, Pallas kernels for 0%

profile of v1, /device:TPU:1, one launch (start us, length us, event | category | flops | bytes accessed | tf_op | source)
XLA Modules:
  0.0 1526.4 jit_solution(14307414345923288356)
XLA Ops:
  9.3 10.8 collective-permute-done.2
  20.2 3.8 collective-permute-start.3
  24.8 7.8 collective-permute-done.3
  32.7 4.3 dynamic_update_slice.11
  37.0 259.0 %while.30 = (s32[]{:T(128)}, f32[512,256]{1,0:T(8,128)S(1)}, f32[16,4,128,256]{3,2,1,0:T(8,128)}, s32[]{:T(128)}, s32[]{:T(128)}, /*index=5*/s32[]{:T(128)}) while((s32[]{:T(128)}, f32[512,256]{1,0:T(8,128)S(1)}, f32[16,4,128,256]{3,2,1,0:T(8,128)}, s32[]{:T(128)}, s32[]{:T(128)}, /*index=5*/s32[]{:T(128)}) %tuple.67), condition=%wide.region_1.2_spmd, body=%wide.region_0.1_spmd.sunk | while | flops 5 | bytes 4194459 | solution.py:53
  37.0 3.5 collective-permute-start
  40.5 15.2 collective-permute-done
  56.6 15.3 collective-permute-done
  72.9 14.3 collective-permute-done
  88.2 14.0 collective-permute-done
  103.2 14.0 collective-permute-done
  118.3 14.0 collective-permute-done
  133.3 14.0 collective-permute-done
  148.3 14.6 collective-permute-done
  163.8 15.6 %collective-permute-done = f32[512,256]{1,0:T(8,128)S(1)} collective-permute-done((f32[512,256]{1,0:T(8,128)S(1)}, f32[512,256]{1,0:T(8,128)S(1)}, u32[]{:S(2)}, u32[]{:S(2)}) %collective-permute-start) | collective-permute-done | bytes 524320 | tf_op jit(solution)/shard_map/while/body/eval_jaxpr/ppermute | solution.py:13
  180.4 16.7 %collective-permute-done = f32[512,256]{1,0:T(8,128)S(1)} collective-permute-done((f32[512,256]{1,0:T(8,128)S(1)}, f32[512,256]{1,0:T(8,128)S(1)}, u32[]{:S(2)}, u32[]{:S(2)}) %collective-permute-start) | collective-permute-done | bytes 524320 | tf_op jit(solution)/shard_map/while/body/eval_jaxpr/ppermute | solution.py:13
  198.1 17.8 %collective-permute-done = f32[512,256]{1,0:T(8,128)S(1)} collective-permute-done((f32[512,256]{1,0:T(8,128)S(1)}, f32[512,256]{1,0:T(8,128)S(1)}, u32[]{:S(2)}, u32[]{:S(2)}) %collective-permute-start) | collective-permute-done | bytes 524320 | tf_op jit(solution)/shard_map/while/body/eval_jaxpr/ppermute | solution.py:13
  216.8 18.9 %collective-permute-done = f32[512,256]{1,0:T(8,128)S(1)} collective-permute-done((f32[512,256]{1,0:T(8,128)S(1)}, f32[512,256]{1,0:T(8,128)S(1)}, u32[]{:S(2)}, u32[]{:S(2)}) %collective-permute-start) | collective-permute-done | bytes 524320 | tf_op jit(solution)/shard_map/while/body/eval_jaxpr/ppermute | solution.py:13
  236.7 19.7 %collective-permute-done = f32[512,256]{1,0:T(8,128)S(1)} collective-permute-done((f32[512,256]{1,0:T(8,128)S(1)}, f32[512,256]{1,0:T(8,128)S(1)}, u32[]{:S(2)}, u32[]{:S(2)}) %collective-permute-start) | collective-permute-done | bytes 524320 | tf_op jit(solution)/shard_map/while/body/eval_jaxpr/ppermute | solution.py:13
  257.4 18.8 %collective-permute-done = f32[512,256]{1,0:T(8,128)S(1)} collective-permute-done((f32[512,256]{1,0:T(8,128)S(1)}, f32[512,256]{1,0:T(8,128)S(1)}, u32[]{:S(2)}, u32[]{:S(2)}) %collective-permute-start) | collective-permute-done | bytes 524320 | tf_op jit(solution)/shard_map/while/body/eval_jaxpr/ppermute | solution.py:13
  277.1 17.8 %collective-permute-done = f32[512,256]{1,0:T(8,128)S(1)} collective-permute-done((f32[512,256]{1,0:T(8,128)S(1)}, f32[512,256]{1,0:T(8,128)S(1)}, u32[]{:S(2)}, u32[]{:S(2)}) %collective-permute-start) | collective-permute-done | bytes 524320 | tf_op jit(solution)/shard_map/while/body/eval_jaxpr/ppermute | solution.py:13
  296.0 13.0 fusion
  311.8 55.4 %reduce-scatter.3.cloned.1.call-done = f32[128,256]{1,0:T(8,128)} async-done(((f32[512,256]{1,0:T(8,128)}), f32[128,256]{1,0:T(8,128)}) %reduce-scatter.3.cloned.1.call-update) | async-done | bytes 131088 | tf_op jit(solution)/shard_map/reduce_scatter | solution.py:58
  369.5 13.7 all_gather.3
  387.1 5.9 convolution_bitcast_fusion
  393.6 2.6 copy-done.2
  396.2 242.4 %while.31 = (s32[]{:T(128)}, f32[512,256]{1,0:T(8,128)S(1)}, f32[16,4,128,256]{3,0,2,1:T(8,128)}, s32[]{:T(128)}, s32[]{:T(128)}, /*index=5*/s32[]{:T(128)}, s32[]{:T(128)}) while((s32[]{:T(128)}, f32[512,256]{1,0:T(8,128)S(1)}, f32[16,4,128,256]{3,0,2,1:T(8,128)}, s32[]{:T(128)}, s32[]{:T(128)}, /*index=5*/s32[]{:T(128)}, s32[]{:T(128)}) %tuple.83), condition=%wide.region_4.5_spmd, body=%wide.region_3.4_spmd.sunk | while | flops 131078 | bytes 5767335 | solution.py:88
  396.2 3.8 collective-permute-start.1
  400.0 2.5 constant_dynamic-slice_fusion.2
  402.6 8.6 collective-permute-done.1
  411.3 8.3 collective-permute-start.1
  422.2 7.7 collective-permute-done.1
  429.9 8.3 collective-permute-start.1
  438.2 2.5 constant_dynamic-slice_fusion.2
  440.8 6.7 collective-permute-done.1
  447.6 8.3 collective-permute-start.1
  455.9 2.5 constant_dynamic-slice_fusion.2
  458.5 5.8 collective-permute-done.1
  464.4 8.3 collective-permute-start.1
  475.3 4.9 collective-permute-done.1
  480.3 8.3 collective-permute-start.1
  491.2 4.0 collective-permute-done.1
  495.3 8.3 collective-permute-start.1
  506.1 3.5 collective-permute-done.1
  509.8 8.0 collective-permute-start.1
  520.4 3.5 collective-permute-done.1
  524.0 8.0 collective-permute-start.1
  534.6 3.5 collective-permute-done.1
  538.2 8.0 collective-permute-start.1
  548.8 3.5 collective-permute-done.1
  552.4 8.0 collective-permute-start.1
  563.0 4.4 collective-permute-done.1
  567.5 8.0 collective-permute-start.1
  578.1 5.5 collective-permute-done.1
  583.7 8.0 collective-permute-start.1
  594.2 6.6 collective-permute-done.1
  600.9 8.0 collective-permute-start.1
  611.5 7.6 collective-permute-done.1
  619.2 8.0 collective-permute-start.1
  629.8 8.7 collective-permute-done.1
  638.7 8.3 collective-permute-done.4
  648.4 645.7 %all-reduce.4.cloned.1.call-done = f32[256,256]{1,0:T(8,128)} async-done(((f32[256,256]{1,0:T(8,128)}), f32[256,256]{1,0:T(8,128)}) %all-reduce.4.cloned.1.call-update) | async-done | bytes 262160 | tf_op jit(solution)/shard_map/psum | solution.py:68
  1295.1 159.4 %psum.30 = f32[256]{0:T(256)S(1)} all-reduce(f32[256]{0:T(256)S(1)} %broadcast_multiply_fusion), channel_id=1, replica_groups=mesh['blk'=64,'rep'=4] {'blk'}, use_global_device_ids=true, to_apply=%region_9.10 | all-reduce | flops 256 | bytes 2048 | tf_op jit(solution)/shard_map/psum | solution.py:68
  1454.5 63.7 %psum.31 = f32[256]{0:T(256)} all-reduce(f32[256]{0:T(256)S(1)} %psum.30), channel_id=1, replica_groups=mesh['blk'=64,'rep'=4] {'rep'}, use_global_device_ids=true, to_apply=%region_10.11 | all-reduce | flops 256 | bytes 2048 | tf_op jit(solution)/shard_map/psum | solution.py:68
  (128 shorter events, 63.1 us)
Async XLA Ops:
  7.2 301.9 %copy-start = (f32[4,4,128,128]{3,2,1,0:T(8,128)S(1)}, f32[4,4,128,128]{3,2,1,0:T(8,128)}, u32[]{:S(2)}) copy-start(f32[4,4,128,128]{3,2,1,0:T(8,128)} %param.11) | copy-start | bytes 3145732
  7.2 360.0 %reduce-scatter.3.cloned.1.call-start = ((), (), s32[]{:S(2)}) async-start(), calls=%async_computation.2 | async-start | bytes 655360 | tf_op jit(solution)/shard_map/reduce_scatter | solution.py:58
  7.2 12.9 collective-permute-start.2
  20.2 12.4 collective-permute-start.3
  37.0 18.7 %collective-permute-start = (f32[512,256]{1,0:T(8,128)S(1)}, f32[512,256]{1,0:T(8,128)S(1)}, u32[]{:S(2)}, u32[]{:S(2)}) collective-permute-start(f32[512,256]{1,0:T(8,128)S(1)} %get-tuple-element.223), channel_id=1, source_target_pairs={{0,4},{4,8},{8,12},{12,16},{16,20},{20,24},{24,28},{28,32},{32,36}... | collective-permute-start | bytes 1572872 | tf_op jit(solution)/shard_map/while/body/eval_jaxpr/ppermute | solution.py:13
  56.5 15.4 %collective-permute-start = (f32[512,256]{1,0:T(8,128)S(1)}, f32[512,256]{1,0:T(8,128)S(1)}, u32[]{:S(2)}, u32[]{:S(2)}) collective-permute-start(f32[512,256]{1,0:T(8,128)S(1)} %get-tuple-element.223), channel_id=1, source_target_pairs={{0,4},{4,8},{8,12},{12,16},{16,20},{20,24},{24,28},{28,32},{32,36}... | collective-permute-start | bytes 1572872 | tf_op jit(solution)/shard_map/while/body/eval_jaxpr/ppermute | solution.py:13
  72.8 14.4 collective-permute-start
  88.1 14.1 collective-permute-start
  103.1 14.1 collective-permute-start
  118.2 14.1 collective-permute-start
  133.2 14.1 collective-permute-start
  148.2 14.6 collective-permute-start
  163.7 15.7 %collective-permute-start = (f32[512,256]{1,0:T(8,128)S(1)}, f32[512,256]{1,0:T(8,128)S(1)}, u32[]{:S(2)}, u32[]{:S(2)}) collective-permute-start(f32[512,256]{1,0:T(8,128)S(1)} %get-tuple-element.223), channel_id=1, source_target_pairs={{0,4},{4,8},{8,12},{12,16},{16,20},{20,24},{24,28},{28,32},{32,36}... | collective-permute-start | bytes 1572872 | tf_op jit(solution)/shard_map/while/body/eval_jaxpr/ppermute | solution.py:13
  180.3 16.8 %collective-permute-start = (f32[512,256]{1,0:T(8,128)S(1)}, f32[512,256]{1,0:T(8,128)S(1)}, u32[]{:S(2)}, u32[]{:S(2)}) collective-permute-start(f32[512,256]{1,0:T(8,128)S(1)} %get-tuple-element.223), channel_id=1, source_target_pairs={{0,4},{4,8},{8,12},{12,16},{16,20},{20,24},{24,28},{28,32},{32,36}... | collective-permute-start | bytes 1572872 | tf_op jit(solution)/shard_map/while/body/eval_jaxpr/ppermute | solution.py:13
  198.0 17.9 %collective-permute-start = (f32[512,256]{1,0:T(8,128)S(1)}, f32[512,256]{1,0:T(8,128)S(1)}, u32[]{:S(2)}, u32[]{:S(2)}) collective-permute-start(f32[512,256]{1,0:T(8,128)S(1)} %get-tuple-element.223), channel_id=1, source_target_pairs={{0,4},{4,8},{8,12},{12,16},{16,20},{20,24},{24,28},{28,32},{32,36}... | collective-permute-start | bytes 1572872 | tf_op jit(solution)/shard_map/while/body/eval_jaxpr/ppermute | solution.py:13
  216.8 19.0 %collective-permute-start = (f32[512,256]{1,0:T(8,128)S(1)}, f32[512,256]{1,0:T(8,128)S(1)}, u32[]{:S(2)}, u32[]{:S(2)}) collective-permute-start(f32[512,256]{1,0:T(8,128)S(1)} %get-tuple-element.223), channel_id=1, source_target_pairs={{0,4},{4,8},{8,12},{12,16},{16,20},{20,24},{24,28},{28,32},{32,36}... | collective-permute-start | bytes 1572872 | tf_op jit(solution)/shard_map/while/body/eval_jaxpr/ppermute | solution.py:13
  236.6 19.7 %collective-permute-start = (f32[512,256]{1,0:T(8,128)S(1)}, f32[512,256]{1,0:T(8,128)S(1)}, u32[]{:S(2)}, u32[]{:S(2)}) collective-permute-start(f32[512,256]{1,0:T(8,128)S(1)} %get-tuple-element.223), channel_id=1, source_target_pairs={{0,4},{4,8},{8,12},{12,16},{16,20},{20,24},{24,28},{28,32},{32,36}... | collective-permute-start | bytes 1572872 | tf_op jit(solution)/shard_map/while/body/eval_jaxpr/ppermute | solution.py:13
  257.3 18.9 %collective-permute-start = (f32[512,256]{1,0:T(8,128)S(1)}, f32[512,256]{1,0:T(8,128)S(1)}, u32[]{:S(2)}, u32[]{:S(2)}) collective-permute-start(f32[512,256]{1,0:T(8,128)S(1)} %get-tuple-element.223), channel_id=1, source_target_pairs={{0,4},{4,8},{8,12},{12,16},{16,20},{20,24},{24,28},{28,32},{32,36}... | collective-permute-start | bytes 1572872 | tf_op jit(solution)/shard_map/while/body/eval_jaxpr/ppermute | solution.py:13
  277.0 17.9 %collective-permute-start = (f32[512,256]{1,0:T(8,128)S(1)}, f32[512,256]{1,0:T(8,128)S(1)}, u32[]{:S(2)}, u32[]{:S(2)}) collective-permute-start(f32[512,256]{1,0:T(8,128)S(1)} %get-tuple-element.223), channel_id=1, source_target_pairs={{0,4},{4,8},{8,12},{12,16},{16,20},{20,24},{24,28},{28,32},{32,36}... | collective-permute-start | bytes 1572872 | tf_op jit(solution)/shard_map/while/body/eval_jaxpr/ppermute | solution.py:13
  296.0 71.2 %copy-start.1 = (f32[128,256]{1,0:T(8,128)S(1)}, f32[128,256]{1,0:T(8,128)}, u32[]{:S(2)}) copy-start(f32[128,256]{1,0:T(8,128)} %param.15) | copy-start | bytes 393220
  296.0 71.2 %copy-start.3 = (f32[256,256]{1,0:T(8,128)S(1)}, f32[256,256]{1,0:T(8,128)}, u32[]{:S(2)}) copy-start(f32[256,256]{1,0:T(8,128)} %param.13) | copy-start | bytes 786436
  296.0 71.2 %copy-start.5 = (f32[256]{0:T(256)S(1)}, f32[256]{0:T(256)}, u32[]{:S(2)}) copy-start(f32[256]{0:T(256)} %param.14) | copy-start | bytes 3076
  311.5 982.6 %all-reduce.4.cloned.1.call-start = ((), (), s32[]{:S(2)}) async-start(), calls=%async_computation.4 | async-start | bytes 524288 | tf_op jit(solution)/shard_map/psum | solution.py:68
  393.0 3.2 copy-start.2
  396.2 251.0 %copy-start.4 = (f32[128,256]{1,0:T(8,128)S(1)}, f32[128,256]{1,0:T(8,128)}, u32[]{:S(2)}) copy-start(f32[128,256]{1,0:T(8,128)} %reduce-scatter.3.cloned.1.call-done) | copy-start | bytes 393220
  396.2 14.9 collective-permute-start.1
  411.3 18.6 %collective-permute-start.1 = (f32[512,256]{1,0:T(8,128)S(1)}, f32[512,256]{1,0:T(8,128)S(1)}, u32[]{:S(2)}, u32[]{:S(2)}) collective-permute-start(f32[512,256]{1,0:T(8,128)S(1)} %get-tuple-element.242), channel_id=1, source_target_pairs={{0,252},{4,0},{8,4},{12,8},{16,12},{20,16},{24,20},{28,24},{32,28}... | collective-permute-start | bytes 1572872 | tf_op jit(solution)/shard_map/while/body/eval_jaxpr/ppermute | solution.py:13
  429.9 17.6 %collective-permute-start.1 = (f32[512,256]{1,0:T(8,128)S(1)}, f32[512,256]{1,0:T(8,128)S(1)}, u32[]{:S(2)}, u32[]{:S(2)}) collective-permute-start(f32[512,256]{1,0:T(8,128)S(1)} %get-tuple-element.242), channel_id=1, source_target_pairs={{0,252},{4,0},{8,4},{12,8},{16,12},{20,16},{24,20},{28,24},{32,28}... | collective-permute-start | bytes 1572872 | tf_op jit(solution)/shard_map/while/body/eval_jaxpr/ppermute | solution.py:13
  447.6 16.7 %collective-permute-start.1 = (f32[512,256]{1,0:T(8,128)S(1)}, f32[512,256]{1,0:T(8,128)S(1)}, u32[]{:S(2)}, u32[]{:S(2)}) collective-permute-start(f32[512,256]{1,0:T(8,128)S(1)} %get-tuple-element.242), channel_id=1, source_target_pairs={{0,252},{4,0},{8,4},{12,8},{16,12},{20,16},{24,20},{28,24},{32,28}... | collective-permute-start | bytes 1572872 | tf_op jit(solution)/shard_map/while/body/eval_jaxpr/ppermute | solution.py:13
  464.4 15.8 %collective-permute-start.1 = (f32[512,256]{1,0:T(8,128)S(1)}, f32[512,256]{1,0:T(8,128)S(1)}, u32[]{:S(2)}, u32[]{:S(2)}) collective-permute-start(f32[512,256]{1,0:T(8,128)S(1)} %get-tuple-element.242), channel_id=1, source_target_pairs={{0,252},{4,0},{8,4},{12,8},{16,12},{20,16},{24,20},{28,24},{32,28}... | collective-permute-start | bytes 1572872 | tf_op jit(solution)/shard_map/while/body/eval_jaxpr/ppermute | solution.py:13
  480.3 14.9 collective-permute-start.1
  495.3 14.4 collective-permute-start.1
  509.8 14.1 collective-permute-start.1
  524.0 14.1 collective-permute-start.1
  538.2 14.1 collective-permute-start.1
  552.4 15.0 collective-permute-start.1
  567.5 16.1 %collective-permute-start.1 = (f32[512,256]{1,0:T(8,128)S(1)}, f32[512,256]{1,0:T(8,128)S(1)}, u32[]{:S(2)}, u32[]{:S(2)}) collective-permute-start(f32[512,256]{1,0:T(8,128)S(1)} %get-tuple-element.242), channel_id=1, source_target_pairs={{0,252},{4,0},{8,4},{12,8},{16,12},{20,16},{24,20},{28,24},{32,28}... | collective-permute-start | bytes 1572872 | tf_op jit(solution)/shard_map/while/body/eval_jaxpr/ppermute | solution.py:13
  583.7 17.2 %collective-permute-start.1 = (f32[512,256]{1,0:T(8,128)S(1)}, f32[512,256]{1,0:T(8,128)S(1)}, u32[]{:S(2)}, u32[]{:S(2)}) collective-permute-start(f32[512,256]{1,0:T(8,128)S(1)} %get-tuple-element.242), channel_id=1, source_target_pairs={{0,252},{4,0},{8,4},{12,8},{16,12},{20,16},{24,20},{28,24},{32,28}... | collective-permute-start | bytes 1572872 | tf_op jit(solution)/shard_map/while/body/eval_jaxpr/ppermute | solution.py:13
  600.9 18.2 %collective-permute-start.1 = (f32[512,256]{1,0:T(8,128)S(1)}, f32[512,256]{1,0:T(8,128)S(1)}, u32[]{:S(2)}, u32[]{:S(2)}) collective-permute-start(f32[512,256]{1,0:T(8,128)S(1)} %get-tuple-element.242), channel_id=1, source_target_pairs={{0,252},{4,0},{8,4},{12,8},{16,12},{20,16},{24,20},{28,24},{32,28}... | collective-permute-start | bytes 1572872 | tf_op jit(solution)/shard_map/while/body/eval_jaxpr/ppermute | solution.py:13
  619.2 19.3 %collective-permute-start.1 = (f32[512,256]{1,0:T(8,128)S(1)}, f32[512,256]{1,0:T(8,128)S(1)}, u32[]{:S(2)}, u32[]{:S(2)}) collective-permute-start(f32[512,256]{1,0:T(8,128)S(1)} %get-tuple-element.242), channel_id=1, source_target_pairs={{0,252},{4,0},{8,4},{12,8},{16,12},{20,16},{24,20},{28,24},{32,28}... | collective-permute-start | bytes 1572872 | tf_op jit(solution)/shard_map/while/body/eval_jaxpr/ppermute | solution.py:13
  638.6 8.4 collective-permute-start.4
  647.1 647.1 %collective-permute-start.5 = (f32[512,256]{1,0:T(8,128)S(1)}, f32[512,256]{1,0:T(8,128)S(1)}, u32[]{:S(2)}, u32[]{:S(2)}) collective-permute-start(f32[512,256]{1,0:T(8,128)S(1)} %broadcast_select_fusion), channel_id=1, source_target_pairs={{0,128},{4,132},{8,136},{12,140},{16,144},{20,148},{24,152},{28,15... | collective-permute-start | bytes 1572872 | tf_op jit(solution)/shard_map/ppermute | solution.py:13
  648.4 869.9 %all-reduce.6.cloned.1.call-start = ((), (), s32[]{:S(2)}) async-start(), calls=%async_computation.5 | async-start | bytes 524288 | tf_op jit(solution)/shard_map/psum | solution.py:68
  1294.2 224.1 %reduce-scatter.5.cloned.1.call-start = ((), (), s32[]{:S(2)}) async-start(), calls=%async_computation.3 | async-start | bytes 655360 | tf_op jit(solution)/shard_map/reduce_scatter | solution.py:92
Sparse Core Ops, SparseCore 0:
  311.6 55.4 reduce-scatter.2
  648.5 645.6 all-reduce.3
  1296.8 79.2 all-reduce.5
  1379.5 34.7 reduce-scatter.4
